TPU v7x, 256 devices: a whole 4x4x8 slice. The times are simulated.
256 devices in a mesh: cfg: 2 (over x_hi), seq: 64 (over x_lo, z, y), clip: 2 (over core).
Axes of the slice: x: 4 (x_hi: 2, x_lo: 2; x = x_hi * 2 + x_lo), y: 4, z: 8, core: 2. Of those that a mesh axis runs over, the one named last changes fastest.
Arguments:
- clean: bfloat16 [128, 256, 1152], P(('clip', 'seq')), parts along dimension 0, may hold values from -6 to 6
- noise: bfloat16 [128, 256, 1152], P(('clip', 'seq')), parts along dimension 0, may hold values from -6 to 6
- timestep: float32 [2], P('clip'), parts along dimension 0, may hold values from 0.1 to 0.9
- guidance: float32 [2], P('clip'), parts along dimension 0, may hold values from 2 to 6
- condition_vector: bfloat16 [2304], P('clip'), parts along dimension 0, may hold values from -6 to 6
- empty_prompt_vector: bfloat16 [1152], replicated, may hold values from -6 to 6
- timestep_direction: bfloat16 [1152], replicated, may hold values from -6 to 6
- spatial_query_key_value: bfloat16 [3, 1152, 1152], P(None, None, ('cfg', 'seq')), may hold values from -1 to 1
- spatial_output_weight: bfloat16 [1152, 1152], P(('cfg', 'seq')), may hold values from -0.1875 to 0.1875
- temporal_query_key_value: bfloat16 [3, 1152, 1152], P(None, None, ('cfg', 'seq')), may hold values from -1 to 1
- temporal_output_weight: bfloat16 [1152, 1152], P(('cfg', 'seq')), may hold values from -0.1875 to 0.1875
- adapter_down_maps: bfloat16 [2, 1152, 64], replicated, may hold values from -0.1875 to 0.1875
- adapter_up_maps: bfloat16 [2, 64, 1152], replicated, may hold values from -0.75 to 0.75
Outputs:
- student_out: bfloat16 [128, 256, 1152], P(('clip', 'seq'), 'cfg'), parts along dimension 0
- student_tangent: bfloat16 [128, 256, 1152], P(('clip', 'seq'), 'cfg'), parts along dimension 0
There are 2 independent parts, one for each index of `clip`. A program takes and returns all parts, laid end to end along the dimension named above; an argument that names none is the same for every part. Nothing has to cross between parts.
All inputs are finite; a program needn't handle non-finite values.
Results may differ from a plain program's by a relative error of at most 0.028.
Values may be sent and summed in bfloat16 or wider, within the bound.
A program may use at most 128 MiB of HBM per device.

v0:
```python
import jax
import jax.numpy as jnp
from jax import lax
from jax.sharding import PartitionSpec as P

HEAD_DIM = 72
epsilon = 1e-06


def partner(value, axis, bit):
    mask = 2**bit
    pairs = [(source, source ^ mask) for source in range(lax.axis_size(axis))]
    return lax.ppermute(value, axis, pairs)


def rms_scale(features):
    return features * lax.rsqrt(jnp.mean(features * features, axis=-1, keepdims=True) + epsilon)


def project(rows_in, matrix):
    return jnp.einsum("...d,dk->...k", rows_in, matrix, preferred_element_type=jnp.float32)


def space_attend(queries, key_rows, value_rows):
    head_count = queries.shape[-1] // HEAD_DIM
    split_dims = queries.shape[:-1] + (head_count, HEAD_DIM)
    scores = jnp.einsum(
        "...qhd,...khd->...hqk",
        queries.reshape(split_dims),
        key_rows.reshape(split_dims),
        preferred_element_type=jnp.float32,
    ) * HEAD_DIM ** (-0.5)
    scores = scores - jnp.max(scores, axis=-1, keepdims=True)
    exponent = jnp.exp(scores)
    soft_weights = (exponent / jnp.sum(exponent, axis=-1, keepdims=True)).astype(jnp.bfloat16)
    result = jnp.einsum(
        "...hqk,...khd->...qhd",
        soft_weights,
        value_rows.reshape(split_dims),
        preferred_element_type=jnp.float32,
    )
    return result.astype(jnp.bfloat16).reshape(queries.shape)


def time_attend(queries, key_rows, value_rows):
    head_count = queries.shape[-1] // HEAD_DIM
    split_dims = queries.shape[:-1] + (head_count, HEAD_DIM)
    scores = jnp.einsum(
        "...fxhd,...gxhd->...xhfg",
        queries.reshape(split_dims),
        key_rows.reshape(split_dims),
        preferred_element_type=jnp.float32,
    ) * HEAD_DIM ** (-0.5)
    scores = scores - jnp.max(scores, axis=-1, keepdims=True)
    exponent = jnp.exp(scores)
    soft_weights = (exponent / jnp.sum(exponent, axis=-1, keepdims=True)).astype(jnp.bfloat16)
    result = jnp.einsum(
        "...xhfg,...gxhd->...fxhd",
        soft_weights,
        value_rows.reshape(split_dims),
        preferred_element_type=jnp.float32,
    )
    return result.astype(jnp.bfloat16).reshape(queries.shape)


def time_core(embedding_rows, query_weight, key_weight, value_weight, out_weight):
    normed = rms_scale(embedding_rows).astype(jnp.bfloat16)
    queries = project(normed, query_weight).astype(jnp.bfloat16)
    key_rows = project(normed, key_weight).astype(jnp.bfloat16)
    value_rows = project(normed, value_weight).astype(jnp.bfloat16)
    return project(time_attend(queries, key_rows, value_rows), out_weight)


def student_network(
    embedding_rows,
    query_weight,
    key_weight,
    value_weight,
    out_weight,
    down_query,
    query_up_map,
    down_value,
    value_up_map,
):
    normed = rms_scale(embedding_rows).astype(jnp.bfloat16)
    low_query = project(normed, down_query).astype(jnp.bfloat16)
    low_value = project(normed, down_value).astype(jnp.bfloat16)
    queries = (project(normed, query_weight) + project(low_query, query_up_map)).astype(
        jnp.bfloat16
    )
    key_rows = project(normed, key_weight).astype(jnp.bfloat16)
    value_rows = (project(normed, value_weight) + project(low_value, value_up_map)).astype(
        jnp.bfloat16
    )
    return project(time_attend(queries, key_rows, value_rows), out_weight)


def on_device(
    clean,
    noise,
    timestep,
    guidance,
    condition_vector,
    empty_prompt_vector,
    timestep_direction,
    spatial_query_key_value,
    spatial_output_weight,
    temporal_query_key_value,
    temporal_output_weight,
    adapter_down_maps,
    adapter_up_maps,
):
    moment = timestep[0]
    strength = guidance[0]
    pair_side = lax.axis_index("cfg")
    noisy_rows = (
        (1.0 - moment) * clean.astype(jnp.float32) + moment * noise.astype(jnp.float32)
    ).astype(jnp.bfloat16)
    shifted = noisy_rows.astype(jnp.float32) + moment * timestep_direction.astype(jnp.float32)
    embeds = jnp.where(pair_side == 0, condition_vector, empty_prompt_vector)[None]
    branch_count = embeds.shape[0]
    entries = shifted[None] + embeds.astype(jnp.float32)[:, None, None, :]
    normed = rms_scale(entries).astype(jnp.bfloat16)
    triple = jnp.einsum(
        "bfpd,jdk->jbfpk",
        normed,
        lax.all_gather(spatial_query_key_value, ("cfg", "seq"), axis=2, tiled=True),
        preferred_element_type=jnp.float32,
    ).astype(jnp.bfloat16)
    attended = space_attend(triple[0], triple[1], triple[2])
    partial_value = jnp.einsum(
        "bfpk,kd->bfpd",
        attended,
        lax.all_gather(spatial_output_weight, ("cfg", "seq"), axis=0, tiled=True),
        preferred_element_type=jnp.float32,
    )
    layer_one = (entries + partial_value).astype(jnp.bfloat16)
    frame_count = layer_one.shape[1]
    position_count = layer_one.shape[2]
    width = layer_one.shape[3]
    stacked = jnp.concatenate([layer_one, noisy_rows[None]], axis=0).reshape(
        branch_count + 1, frame_count, 2, position_count // 2, width
    )
    regrouped = lax.all_to_all(stacked, "seq", split_axis=3, concat_axis=1, tiled=True)
    frames = regrouped.shape[1]
    local_rows = regrouped.shape[3]
    teacher_in = regrouped[:branch_count].reshape(branch_count, frames, 2 * local_rows, width)
    noisy_local = regrouped[branch_count]
    time_qkv, time_out = (
        lax.all_gather(temporal_query_key_value, ("cfg", "seq"), axis=2, tiled=True),
        lax.all_gather(temporal_output_weight, ("cfg", "seq"), axis=0, tiled=True),
    )
    teacher_part = time_core(
        teacher_in.astype(jnp.float32), time_qkv[0], time_qkv[1], time_qkv[2], time_out
    )
    velocity = (
        (teacher_in.astype(jnp.float32) + teacher_part)
        .astype(jnp.bfloat16)
        .reshape(branch_count, frames, 2, local_rows, width)
    )
    own_velocity = velocity[0]
    own_half = lax.dynamic_index_in_dim(own_velocity, pair_side, 1, keepdims=False)
    outgoing = lax.dynamic_index_in_dim(own_velocity, 1 - pair_side, 1, keepdims=False)
    other_half = partner(outgoing, "cfg", 0)
    is_first = pair_side == 0
    cond_velocity = jnp.where(is_first, own_half, other_half)
    uncond_velocity = jnp.where(is_first, other_half, own_half)
    student_noisy = lax.dynamic_index_in_dim(noisy_local, pair_side, 1, keepdims=False)
    query_up_map = adapter_up_maps[0]
    value_up_map = adapter_up_maps[1]
    uncond_float = uncond_velocity.astype(jnp.float32)
    guided = (uncond_float + strength * (cond_velocity.astype(jnp.float32) - uncond_float)).astype(
        jnp.bfloat16
    )
    student_in = (
        student_noisy.astype(jnp.float32)
        + moment * timestep_direction.astype(jnp.float32)
        + condition_vector.astype(jnp.float32)
    )

    def student_map(embedding_rows):
        return student_network(
            embedding_rows,
            time_qkv[0],
            time_qkv[1],
            time_qkv[2],
            time_out,
            adapter_down_maps[0],
            query_up_map,
            adapter_down_maps[1],
            value_up_map,
        )

    partial_value, tangent_part = jax.jvp(student_map, (student_in,), (guided.astype(jnp.float32),))
    primal = (student_in + partial_value).astype(jnp.bfloat16)
    tangent = (guided.astype(jnp.float32) + tangent_part).astype(jnp.bfloat16)
    returned = lax.all_to_all(
        jnp.stack([primal, tangent]), "seq", split_axis=1, concat_axis=2, tiled=True
    )
    return (returned[0], returned[1])


def solution(mesh):
    return jax.shard_map(
        on_device,
        mesh=mesh,
        in_specs=(
            P(("clip", "seq"), None, None),
            P(("clip", "seq"), None, None),
            P("clip"),
            P("clip"),
            P("clip"),
            P(),
            P(),
            P(None, None, ("cfg", "seq")),
            P(("cfg", "seq"), None),
            P(None, None, ("cfg", "seq")),
            P(("cfg", "seq"), None),
            P(),
            P(),
        ),
        out_specs=(P(("clip", "seq"), "cfg", None), P(("clip", "seq"), "cfg", None)),
        check_vma=False,
    )
```

profile of v0, /device:TPU:32, one launch (start us, length us, event | category | flops | bytes accessed | tf_op | source)
XLA Modules:
  0.0 703.8 jit_solution(14930948228672094972)
XLA Ops:
  15.2 115.8 %all-gather.11.cloned.1.call-done = bf16[128,9,1152]{2,1,0:T(8,128)(2,1)} async-done(((bf16[1,9,1152]{2,1,0:T(8,128)(2,1)}), bf16[128,9,1152]{2,1,0:T(8,128)(2,1)}) %all-gather.11.cloned.1.call-update) | async-done | bytes 2654224 | tf_op jit(solution)/shard_map/all_gather | solution.py:134
  131.0 4.3 reshape.305
  135.3 113.3 %all-gather.13.cloned.1.call-done = bf16[128,9,1152]{2,1,0:T(8,128)(2,1)} async-done(((bf16[1,9,1152]{2,1,0:T(8,128)(2,1)}), bf16[128,9,1152]{2,1,0:T(8,128)(2,1)}) %all-gather.13.cloned.1.call-update) | async-done | bytes 2654224 | tf_op jit(solution)/shard_map/all_gather | solution.py:151
  248.6 5.7 reshape.316
  254.4 124.3 %all-gather.7.cloned.1.call-done = bf16[3,1152,1152]{1,0,2:T(4,128)(2,1)} async-done(((bf16[3,1152,9]{1,0,2:T(4,128)(2,1)}), bf16[3,1152,1152]{1,0,2:T(4,128)(2,1)}) %all-gather.7.cloned.1.call-update) | async-done | bytes 7962640 | tf_op jit(solution)/shard_map/all_gather | solution.py:127
  378.7 6.6 fusion.10
  391.9 4.9 fusion.164
  396.8 2.8 fusion.61
  401.3 2.6 pad_maximum_fusion
  403.9 8.9 %all-to-all-start = ((bf16[2,1,2,128,1152]{4,2,0,1,3:T(2,128)(2,1)}), bf16[2,1,2,128,1152]{4,2,0,1,3:T(2,128)(2,1)}, u32[]{:S(2)}, u32[]{:S(2)}) async-start(bf16[2,1,2,128,1152]{4,2,0,1,3:T(2,128)(2,1)} %pad_maximum_fusion), calls=%async_computation | async-start | bytes 2359296 | tf_op jit(solution)/shard_map/all_to_all | solution.py:144
  412.7 98.1 %all-gather.9.cloned.1.call-done = bf16[3,1152,1152]{1,0,2:T(4,128)(2,1)} async-done(((bf16[3,1152,9]{1,0,2:T(4,128)(2,1)}), bf16[3,1152,1152]{1,0,2:T(4,128)(2,1)}) %all-gather.9.cloned.1.call-update) | async-done | bytes 7962640 | tf_op jit(solution)/shard_map/all_gather | solution.py:150
  510.9 24.1 %fusion.161 = (bf16[1,1152,1152]{1,0,2:T(2,128)(2,1)}, bf16[1,1152,1152]{1,0,2:T(2,128)(2,1)}, bf16[1,1152,1152]{1,0,2:T(2,128)(2,1)}) fusion(bf16[3,1152,1152]{1,0,2:T(4,128)(2,1)} %all-gather.9.cloned.1.call-done), kind=kLoop, calls=%fused_computation.171 | loop fusion | bytes 15925248 | tf_op jit(solution)/shard_map/jvp()/slice | solution.py:184
  535.0 10.9 %copy.107 = bf16[1,1152,1152]{2,1,0:T(8,128)(2,1)S(1)} copy(bf16[1,1152,1152]{1,0,2:T(2,128)(2,1)} %get-tuple-element.11) | data formatting | bytes 5308416
  545.8 12.2 %copy.108 = bf16[1,1152,1152]{2,1,0:T(8,128)(2,1)} copy(bf16[1,1152,1152]{1,0,2:T(2,128)(2,1)} %get-tuple-element.13) | data formatting | bytes 5308416
  558.1 12.2 %copy.106 = bf16[1,1152,1152]{2,1,0:T(8,128)(2,1)} copy(bf16[1,1152,1152]{1,0,2:T(2,128)(2,1)} %get-tuple-element.12) | data formatting | bytes 5308416
  574.8 2.8 reshape.295
  577.6 2.9 fusion.37
  580.5 2.8 reshape.296
  583.3 3.6 fusion.66
  586.9 2.6 fusion.165
  589.5 2.5 slice_convert_fusion
  592.1 2.9 fusion.31
  595.0 3.7 reshape.294
  598.7 3.9 fusion.59
  602.6 2.9 copy.88
  605.5 2.9 reshape.297
  608.4 3.2 fusion.41
  613.2 3.1 collective-permute-start
  616.9 5.5 collective-permute-done
  623.8 3.4 fusion.29
  655.0 2.3 fusion.55
  667.6 27.1 %all_to_all.24 = bf16[2,64,2,1152]{3,2,0,1:T(2,128)(2,1)S(1)} all-to-all(bf16[2,64,2,1152]{3,2,0,1:T(2,128)(2,1)S(1)} %copy.98), channel_id=1, replica_groups=mesh['cfg'=2,'seq'=64,'clip'=2] {'seq'}, dimensions={1} | all-to-all | bytes 1179648 | tf_op jit(solution)/shard_map/all_to_all | solution.py:197
  (135 shorter events, 62.8 us)
Async XLA Ops:
  7.2 123.8 %all-gather.11.cloned.1.call-start = ((), (), s32[]{:S(2)}) async-start(), calls=%async_computation.4 | async-start | bytes 4755456 | tf_op jit(solution)/shard_map/all_gather | solution.py:134
  7.9 240.7 %all-gather.13.cloned.1.call-start = ((), (), s32[]{:S(2)}) async-start(), calls=%async_computation.5 | async-start | bytes 4755456 | tf_op jit(solution)/shard_map/all_gather | solution.py:151
  8.6 370.0 %all-gather.7.cloned.1.call-start = ((), (), s32[]{:S(2)}) async-start(), calls=%async_computation.2 | async-start | bytes 10699776 | tf_op jit(solution)/shard_map/all_gather | solution.py:127
  9.4 501.5 %all-gather.9.cloned.1.call-start = ((), (), s32[]{:S(2)}) async-start(), calls=%async_computation.3 | async-start | bytes 10699776 | tf_op jit(solution)/shard_map/all_gather | solution.py:150
  13.8 364.9 %copy-start.15 = (bf16[1,256,1152]{2,1,0:T(8,128)(2,1)}, bf16[1,256,1152]{2,1,0:T(8,128)(2,1)S(1)}, u32[]{:S(2)}) copy-start(bf16[1,256,1152]{2,1,0:T(8,128)(2,1)S(1)} %get-tuple-element.10) | copy-start | bytes 1769476
  391.9 4.9 copy-start.22
  396.8 2.8 copy-start.16
  399.6 1.7 copy-start.14
  403.9 166.4 %all-to-all-start = ((bf16[2,1,2,128,1152]{4,2,0,1,3:T(2,128)(2,1)}), bf16[2,1,2,128,1152]{4,2,0,1,3:T(2,128)(2,1)}, u32[]{:S(2)}, u32[]{:S(2)}) async-start(bf16[2,1,2,128,1152]{4,2,0,1,3:T(2,128)(2,1)} %pad_maximum_fusion), calls=%async_computation | async-start | bytes 2359296 | tf_op jit(solution)/shard_map/all_to_all | solution.py:144
  589.5 2.6 copy-start
  613.2 9.2 %collective-permute-start = (bf16[64,2,1152]{2,0,1:T(8,128)(2,1)}, bf16[64,2,1152]{2,0,1:T(8,128)(2,1)S(1)}, u32[]{:S(2)}, u32[]{:S(2)}) collective-permute-start(bf16[64,2,1152]{2,0,1:T(8,128)(2,1)} %dynamic-slice_bitcast_fusion), channel_id=1, source_target_pairs={{0,128},{128,0},{1,129},{129,1},{2,130},{130,2},{3,131},{131,3},{4... | collective-permute-start | bytes 884744 | tf_op jit(solution)/shard_map/ppermute | solution.py:13
  623.8 3.4 copy-start.9
  623.8 7.6 %copy-start.27 = (f32[64,2]{0,1:T(2,128)}, f32[64,2]{0,1:T(2,128)S(1)}, u32[]{:S(2)}) copy-start(f32[64,2]{0,1:T(2,128)S(1)} %get-tuple-element.23) | copy-start | bytes 1540
  623.8 3.6 copy-start.2
  631.4 2.0 copy-start.1
  634.8 4.3 copy-start.13
  637.2 7.1 %copy-start.11 = (f32[64,2,1152]{2,0,1:T(8,128)S(1)}, f32[64,2,1152]{2,0,1:T(8,128)}, u32[]{:S(2)}) copy-start(f32[64,2,1152]{2,0,1:T(8,128)} %fusion.23) | copy-start | bytes 1769476
  648.5 2.6 copy-start.7
  648.6 2.6 copy-start.25
  649.0 2.1 copy-start.23
  649.4 2.1 copy-start.29
  651.1 3.9 copy-start.3
  657.2 3.7 copy-start.26
  657.2 3.7 copy-start.32
  661.0 2.0 copy-start.33
  661.0 2.0 copy-start.6
  661.0 2.0 copy-start.8
  661.0 2.1 copy-start.24
  661.0 2.1 copy-start.30
  661.0 2.1 copy-start.34
  663.1 2.2 copy-start.10
  665.3 1.6 copy-start.19
  (9 other events, 11.0 us)
Sparse Core Ops, SparseCore 0:
  11.7 119.2 all-gather.10
  134.7 113.9 all-gather.12
  252.2 126.4 all-gather.6
  382.1 128.6 all-gather.8
where the time goes:
time: 714 us; the launch traced here: 704 us
  waiting for transfers between devices  460 us (64%)
  local copies, waits for them, and re-layouts  116 us (16%)
  matrix products  60.1 us (8%)
  blocking collectives  27.1 us (4%)
  between operations  16 us (2%)
  other arithmetic  12.3 us (2%)
  starting transfers between devices  12.1 us (2%)
    all_gather x1, waiting for transfers between devices, on_device(): lax.all_gather(spatial_query_key_value, ('cfg', 'seq'), axis=2, tiled=True)  124 us
    all_gather x1, waiting for transfers between devices, on_device(): lax.all_gather(spatial_output_weight, ('cfg', 'seq'), axis=0, tiled=True)  116 us
    all_gather x1, waiting for transfers between devices, on_device(): lax.all_gather(temporal_output_weight, ('cfg', 'seq'), axis=0, tiled=True)  113 us
    all_gather x1, waiting for transfers between devices, on_device(): lax.all_gather(temporal_query_key_value, ('cfg', 'seq'), axis=2, tiled=True)  98.1 us
    unnamed x75, local copies, waits for them, and re-layouts  48.6 us
    dot_general x16, matrix products, project(): jnp.einsum('...d,dk->...k', rows_in, matrix, preferred_element_type=jnp.f...  29.4 us
    all_to_all x1, blocking collectives, on_device(): lax.all_to_all(jnp.stack([primal, tangent]), 'seq', split_axis=1, concat_...  27.1 us
    slice x1, local copies, waits for them, and re-layouts, student_map(): time_qkv[0]  24.1 us
  transfers between devices with their start and end apart: 6, of which 5 were waited for; matrix products, arithmetic and copies ran while one was open for 14% of the time, Pallas kernels for 0%

commit v1 on v0

--- a/solution.py
+++ b/solution.py
@@ -2,6 +2,7 @@
 import jax.numpy as jnp
 from jax import lax
 from jax.sharding import PartitionSpec as P
+from jax.lax import all_to_all, axis_size
 
 HEAD_DIM = 72
 epsilon = 1e-06
@@ -121,10 +122,19 @@
     branch_count = embeds.shape[0]
     entries = shifted[None] + embeds.astype(jnp.float32)[:, None, None, :]
     normed = rms_scale(entries).astype(jnp.bfloat16)
+
+    def _unite_units(arr_in):
+        return jnp.concatenate(
+            all_to_all(
+                jnp.stack([arr_in for _ in range(axis_size(("cfg", "seq")))]), ("cfg", "seq"), 0, 0
+            ),
+            2,
+        )
+
     triple = jnp.einsum(
         "bfpd,jdk->jbfpk",
         normed,
-        lax.all_gather(spatial_query_key_value, ("cfg", "seq"), axis=2, tiled=True),
+        _unite_units(spatial_query_key_value),
         preferred_element_type=jnp.float32,
     ).astype(jnp.bfloat16)
     attended = space_attend(triple[0], triple[1], triple[2])

time: 714 us -> 658 us (0.922)
  waiting for transfers between devices: 460 us -> 391 us
  starting transfers between devices: 12.1 us -> 28.1 us
    all_gather x1 -> x0, waiting for transfers between devices: 124 us -> none  [on_device(): lax.all_gather(spatial_query_key_value, ('cfg', 'seq'), axis=2, tiled=True)]
    all_gather x1, waiting for transfers between devices: 116 us -> 158 us  [on_device(): lax.all_gather(spatial_output_weight, ('cfg', 'seq'), axis=0, tiled=True)]
    all_gather x1, waiting for transfers between devices: 113 us -> 133 us  [on_device(): lax.all_gather(temporal_output_weight, ('cfg', 'seq'), axis=0, tiled=True)]
    all_to_all x0 -> x1, starting transfers between devices: none -> 15.5 us  [_unite_units(): all_to_all(jnp.stack([arr_in for _ in range(axis_size(('cfg', 'seq')))]),...]
    another operation x4 -> x5, local copies, waits for them, and re-layouts: 12.3 us -> 17.6 us
    unnamed x75 -> x85, local copies, waits for them, and re-layouts: 48.6 us -> 48.6 us
  transfers between devices with their start and end apart: 6 -> 6, of which waited for: 5 -> 4; matrix products, arithmetic and copies ran while one was open for 14% -> 16% of each run, Pallas kernels for 0% -> 0%
where the time goes in v1:
time: 658 us; the launch traced here: 654 us
  waiting for transfers between devices  391 us (59%)
  local copies, waits for them, and re-layouts  122 us (19%)
  matrix products  60 us (9%)
  starting transfers between devices  28.1 us (4%)
  blocking collectives  27.2 us (4%)
  between operations  15.9 us (2%)
  other arithmetic  9.71 us (1%)
    all_gather x1, waiting for transfers between devices, on_device(): lax.all_gather(spatial_output_weight, ('cfg', 'seq'), axis=0, tiled=True)  158 us
    all_gather x1, waiting for transfers between devices, on_device(): lax.all_gather(temporal_output_weight, ('cfg', 'seq'), axis=0, tiled=True)  133 us
    all_gather x1, waiting for transfers between devices, on_device(): lax.all_gather(temporal_query_key_value, ('cfg', 'seq'), axis=2, tiled=True)  92.9 us
    unnamed x85, local copies, waits for them, and re-layouts  48.6 us
    dot_general x16, matrix products, project(): jnp.einsum('...d,dk->...k', rows_in, matrix, preferred_element_type=jnp.f...  29.4 us
    all_to_all x1, blocking collectives, on_device(): lax.all_to_all(jnp.stack([primal, tangent]), 'seq', split_axis=1, concat_...  27.2 us
    slice x1, local copies, waits for them, and re-layouts, student_map(): time_qkv[0]  24 us
    all_to_all x1, starting transfers between devices, _unite_units(): all_to_all(jnp.stack([arr_in for _ in range(axis_size(('cfg', 'seq')))]),...  15.5 us
  transfers between devices with their start and end apart: 6, of which 4 were waited for; matrix products, arithmetic and copies ran while one was open for 16% of the time, Pallas kernels for 0%

profile of v1, /device:TPU:32, one launch (start us, length us, event | category | flops | bytes accessed | tf_op | source)
XLA Modules:
  0.0 653.6 jit_solution(17117820065498324245)
XLA Ops:
  8.6 5.3 stack.8
  14.0 15.5 %all-to-all-start = ((bf16[128,3,1152,9]{2,1,3,0:T(4,128)(2,1)}), bf16[128,3,1152,9]{2,1,3,0:T(4,128)(2,1)}, u32[]{:S(2)}, u32[]{:S(2)}) async-start(bf16[128,3,1152,9]{2,1,3,0:T(4,128)(2,1)} %stack.8), calls=%async_computation | async-start | bytes 21233664 | tf_op jit(solution)/shard_map/all_to_all | solution.py:128
  32.9 157.5 %all-gather.8.cloned.1.call-done = bf16[128,9,1152]{2,1,0:T(8,128)(2,1)} async-done(((bf16[1,9,1152]{2,1,0:T(8,128)(2,1)}), bf16[128,9,1152]{2,1,0:T(8,128)(2,1)}) %all-gather.8.cloned.1.call-update) | async-done | bytes 2654224 | tf_op jit(solution)/shard_map/all_gather | solution.py:144
  190.4 4.3 reshape.378
  194.7 133.4 %all-gather.10.cloned.1.call-done = bf16[128,9,1152]{2,1,0:T(8,128)(2,1)} async-done(((bf16[1,9,1152]{2,1,0:T(8,128)(2,1)}), bf16[128,9,1152]{2,1,0:T(8,128)(2,1)}) %all-gather.10.cloned.1.call-update) | async-done | bytes 2654224 | tf_op jit(solution)/shard_map/all_gather | solution.py:161
  328.1 5.7 reshape.389
  333.8 6.6 %fusion.10 = bf16[3,1,1,256,1152]{4,3,0,2,1:T(8,128)(2,1)S(1)} fusion(bf16[3,1152,1152]{1,0,2:T(4,128)(2,1)} %bitcast.6, bf16[1,256,1152]{2,1,0:T(8,128)(2,1)S(1)} %get-tuple-element.10, f32[256]{0:T(256)S(1)} %add_rsqrt_fusion.1, f32[1152]{0:T(1024)S(1)} %get-tuple-element.21, f32[1152]{0:T(1024)S(1)} %convert_multiply_fusion.1), kind=kOutput, calls=%fused_computation.9 | convolution fusion | flops 2040791040 | bytes 10332160 | tf_op jit(solution)/shard_map/bfpd,jdk->jbfpk/dot_general | solution.py:134
  347.0 4.9 fusion.166
  351.9 2.8 fusion.61
  356.4 2.5 pad_maximum_fusion
  358.9 8.8 %all-to-all-start.1 = ((bf16[2,1,2,128,1152]{4,2,0,1,3:T(2,128)(2,1)}), bf16[2,1,2,128,1152]{4,2,0,1,3:T(2,128)(2,1)}, u32[]{:S(2)}, u32[]{:S(2)}) async-start(bf16[2,1,2,128,1152]{4,2,0,1,3:T(2,128)(2,1)} %pad_maximum_fusion), calls=%async_computation.1 | async-start | bytes 2359296 | tf_op jit(solution)/shard_map/all_to_all | solution.py:154
  367.8 92.9 %all-gather.6.cloned.1.call-done = bf16[3,1152,1152]{1,0,2:T(4,128)(2,1)} async-done(((bf16[3,1152,9]{1,0,2:T(4,128)(2,1)}), bf16[3,1152,1152]{1,0,2:T(4,128)(2,1)}) %all-gather.6.cloned.1.call-update) | async-done | bytes 7962640 | tf_op jit(solution)/shard_map/all_gather | solution.py:160
  460.7 24.0 %fusion.163 = (bf16[1,1152,1152]{1,0,2:T(2,128)(2,1)}, bf16[1,1152,1152]{1,0,2:T(2,128)(2,1)}, bf16[1,1152,1152]{1,0,2:T(2,128)(2,1)}) fusion(bf16[3,1152,1152]{1,0,2:T(4,128)(2,1)} %all-gather.6.cloned.1.call-done), kind=kLoop, calls=%fused_computation.173 | loop fusion | bytes 15925248 | tf_op jit(solution)/shard_map/jvp()/slice | solution.py:194
  484.7 10.9 %copy.107 = bf16[1,1152,1152]{2,1,0:T(8,128)(2,1)S(1)} copy(bf16[1,1152,1152]{1,0,2:T(2,128)(2,1)} %get-tuple-element.11) | data formatting | bytes 5308416
  495.6 12.2 %copy.108 = bf16[1,1152,1152]{2,1,0:T(8,128)(2,1)} copy(bf16[1,1152,1152]{1,0,2:T(2,128)(2,1)} %get-tuple-element.13) | data formatting | bytes 5308416
  507.8 12.2 %copy.106 = bf16[1,1152,1152]{2,1,0:T(8,128)(2,1)} copy(bf16[1,1152,1152]{1,0,2:T(2,128)(2,1)} %get-tuple-element.12) | data formatting | bytes 5308416
  524.5 2.8 reshape.368
  527.3 2.9 fusion.37
  530.3 2.9 reshape.369
  533.2 3.6 fusion.68
  536.7 2.6 fusion.167
  539.3 2.6 slice_convert_fusion
  542.0 2.9 fusion.31
  544.8 3.7 reshape.367
  548.5 3.9 fusion.59
  552.4 2.9 copy.88
  555.3 2.9 reshape.370
  558.3 3.2 fusion.41
  563.1 3.1 collective-permute-start
  566.8 5.5 collective-permute-done
  573.7 3.4 fusion.29
  617.6 27.2 %all_to_all.29 = bf16[2,64,2,1152]{3,2,0,1:T(2,128)(2,1)S(1)} all-to-all(bf16[2,64,2,1152]{3,2,0,1:T(2,128)(2,1)S(1)} %copy.98), channel_id=1, replica_groups=mesh['cfg'=2,'seq'=64,'clip'=2] {'seq'}, dimensions={1} | all-to-all | bytes 1179648 | tf_op jit(solution)/shard_map/all_to_all | solution.py:207
  (145 shorter events, 61.9 us)
Async XLA Ops:
  7.2 183.2 %all-gather.8.cloned.1.call-start = ((), (), s32[]{:S(2)}) async-start(), calls=%async_computation.4 | async-start | bytes 4755456 | tf_op jit(solution)/shard_map/all_gather | solution.py:144
  7.9 320.2 %all-gather.10.cloned.1.call-start = ((), (), s32[]{:S(2)}) async-start(), calls=%async_computation.5 | async-start | bytes 4755456 | tf_op jit(solution)/shard_map/all_gather | solution.py:161
  13.9 17.0 %copy-start.37 = (bf16[1152]{0:T(1024)(128)(2,1)S(1)}, bf16[1152]{0:T(1024)(128)(2,1)}, u32[]{:S(2)}) copy-start(bf16[1152]{0:T(1024)(128)(2,1)} %param.19) | copy-start | bytes 6916
  13.9 17.0 %copy-start.38 = (bf16[1152]{0:T(1024)(128)(2,1)S(1)}, bf16[1152]{0:T(1024)(128)(2,1)}, u32[]{:S(2)}) copy-start(bf16[1152]{0:T(1024)(128)(2,1)} %param.17) | copy-start | bytes 6916
  13.9 17.0 %copy-start.39 = (bf16[1152]{0:T(1024)(128)(2,1)S(1)}, bf16[1152]{0:T(1024)(128)(2,1)}, u32[]{:S(2)}) copy-start(bf16[1152]{0:T(1024)(128)(2,1)} %param.18) | copy-start | bytes 6916
  13.9 17.0 %copy-start.23 = (bf16[1,256,1152]{2,1,0:T(8,128)(2,1)S(1)}, bf16[1,256,1152]{2,1,0:T(8,128)(2,1)}, u32[]{:S(2)}) copy-start(bf16[1,256,1152]{2,1,0:T(8,128)(2,1)} %param.14) | copy-start | bytes 1769476
  14.0 17.0 %copy-start.24 = (bf16[1,256,1152]{2,1,0:T(8,128)(2,1)S(1)}, bf16[1,256,1152]{2,1,0:T(8,128)(2,1)}, u32[]{:S(2)}) copy-start(bf16[1,256,1152]{2,1,0:T(8,128)(2,1)} %param.13) | copy-start | bytes 1769476
  14.0 319.9 %all-to-all-start = ((bf16[128,3,1152,9]{2,1,3,0:T(4,128)(2,1)}), bf16[128,3,1152,9]{2,1,3,0:T(4,128)(2,1)}, u32[]{:S(2)}, u32[]{:S(2)}) async-start(bf16[128,3,1152,9]{2,1,3,0:T(4,128)(2,1)} %stack.8), calls=%async_computation | async-start | bytes 21233664 | tf_op jit(solution)/shard_map/all_to_all | solution.py:128
  29.5 431.2 %all-gather.6.cloned.1.call-start = ((), (), s32[]{:S(2)}) async-start(), calls=%async_computation.3 | async-start | bytes 10699776 | tf_op jit(solution)/shard_map/all_gather | solution.py:160
  31.4 302.4 %copy-start.15 = (bf16[1,256,1152]{2,1,0:T(8,128)(2,1)}, bf16[1,256,1152]{2,1,0:T(8,128)(2,1)S(1)}, u32[]{:S(2)}) copy-start(bf16[1,256,1152]{2,1,0:T(8,128)(2,1)S(1)} %get-tuple-element.10) | copy-start | bytes 1769476
  347.0 4.9 copy-start.22
  351.9 2.8 copy-start.16
  358.9 161.1 %all-to-all-start.1 = ((bf16[2,1,2,128,1152]{4,2,0,1,3:T(2,128)(2,1)}), bf16[2,1,2,128,1152]{4,2,0,1,3:T(2,128)(2,1)}, u32[]{:S(2)}, u32[]{:S(2)}) async-start(bf16[2,1,2,128,1152]{4,2,0,1,3:T(2,128)(2,1)} %pad_maximum_fusion), calls=%async_computation.1 | async-start | bytes 2359296 | tf_op jit(solution)/shard_map/all_to_all | solution.py:154
  539.3 2.7 copy-start
  563.1 9.2 %collective-permute-start = (bf16[64,2,1152]{2,0,1:T(8,128)(2,1)}, bf16[64,2,1152]{2,0,1:T(8,128)(2,1)S(1)}, u32[]{:S(2)}, u32[]{:S(2)}) collective-permute-start(bf16[64,2,1152]{2,0,1:T(8,128)(2,1)} %dynamic-slice_bitcast_fusion), channel_id=1, source_target_pairs={{0,128},{128,0},{1,129},{129,1},{2,130},{130,2},{3,131},{131,3},{4... | collective-permute-start | bytes 884744 | tf_op jit(solution)/shard_map/ppermute | solution.py:14
  573.7 3.4 copy-start.9
  573.7 7.6 %copy-start.29 = (f32[64,2]{0,1:T(2,128)}, f32[64,2]{0,1:T(2,128)S(1)}, u32[]{:S(2)}) copy-start(f32[64,2]{0,1:T(2,128)S(1)} %get-tuple-element.23) | copy-start | bytes 1540
  573.7 3.6 copy-start.2
  584.7 4.3 copy-start.13
  587.1 7.1 %copy-start.11 = (f32[64,2,1152]{2,0,1:T(8,128)S(1)}, f32[64,2,1152]{2,0,1:T(8,128)}, u32[]{:S(2)}) copy-start(f32[64,2,1152]{2,0,1:T(8,128)} %fusion.23) | copy-start | bytes 1769476
  598.5 2.6 copy-start.7
  598.5 2.6 copy-start.27
  598.9 2.1 copy-start.25
  599.3 2.1 copy-start.31
  601.0 3.9 copy-start.3
  607.2 3.7 copy-start.28
  607.2 3.7 copy-start.34
  610.9 2.0 copy-start.8
  610.9 2.1 copy-start.26
  610.9 2.1 copy-start.32
  610.9 2.1 copy-start.36
  613.1 2.2 copy-start.10
  (14 other events, 20.2 us)
Sparse Core Ops, SparseCore 0:
  11.7 178.6 all-gather.7
  194.1 133.9 all-gather.9
  331.7 128.9 all-gather.5
